TPU v7x, 32 devices: a whole 2x2x4 slice. The times are simulated.
32 devices in a mesh: row: 8 (over z, core), col: 4 (over y, x).
Axes of the slice: x: 2, y: 2, z: 4, core: 2. Of those that a mesh axis runs over, the one named last changes fastest.
Arguments:
- radar_field: float32 [64, 64, 384], P('row', 'col'), may hold values from -6 to 6
- kernels: bfloat16 [2, 2, 3, 3, 384, 384], P(None, None, None, None, None, 'row'), may hold values from -0.109375 to 0.109375
- norm_gain_weights: float32 [2, 384], replicated, may hold values from 0.25 to 1.75
Outputs:
- field_out: float32 [64, 64, 384], P('row', 'col')
All inputs are finite; a program needn't handle non-finite values.
Results may differ from a plain program's by a relative error of at most 0.0032.
Values may be sent and summed in bfloat16 or wider, within the bound.
A program may use at most 64 MiB of HBM per device.

v0:
```python
import jax
import jax.numpy as jnp
from jax import lax
from jax.sharding import PartitionSpec as P

BLOCKS = 2
FIRST_DILATION = 32
SECOND_DILATION = 64


norm_floor = 1e-06


def passed_along(value, axis, steps):
    count = lax.axis_size(axis)
    initial, last = (max(0, -steps), min(count, count - steps))
    return lax.ppermute(value, axis, [(source, source + steps) for source in range(initial, last)])


def extended(cells, sides, width):
    for axis, dim in sides:
        count = lax.axis_size(axis)
        ends = count - 1
        head = lax.slice_in_dim(cells, 0, width, axis=dim)
        tail = lax.slice_in_dim(cells, cells.shape[dim] - width, cells.shape[dim], axis=dim)
        cells = jnp.concatenate(
            [
                lax.ppermute(tail, axis, [(i, (i + 1) % count) for i in range(ends)]),
                cells,
                lax.ppermute(head, axis, [((i + 1) % count, i) for i in range(ends)]),
            ],
            axis=dim,
        )
    return cells


def row_direction(stacked, tap_displacement):
    moved = {}
    for side in (-1, 1):
        moved[side] = passed_along(stacked, "row", -side * tap_displacement)
    return moved


def along_cols(stacked, tap_displacement):
    moved = {}
    for side in (-1, 1):
        moved[side] = passed_along(stacked, "col", -side * tap_displacement)
    return moved


def dilated_taps(cast_state, row_step, col_step):
    tap_list = []
    row_moved = row_direction(cast_state, row_step)
    centre = jnp.stack([row_moved[-1], cast_state, row_moved[1]])
    col_moved = along_cols(centre, col_step)
    for row_off in (-1, 0, 1):
        for col_off in (-1, 0, 1):
            if col_off == 0:
                tap_list.append(centre[row_off + 1])
            else:
                tap_list.append(col_moved[col_off][row_off + 1])
    return jnp.stack(tap_list)


def contract(tap_stack, kernel_part):
    channels = tap_stack.shape[-1]
    flat_taps = tap_stack.reshape(9, -1, channels)
    flat_kernel = kernel_part.reshape(9, channels, -1)
    return lax.dot_general(
        flat_taps, flat_kernel, (((0, 2), (0, 1)), ((), ())), preferred_element_type=jnp.float32
    )


def convolve(tap_stack, kernels, block_index, which):
    gathered = lax.all_gather(kernels[block_index, which], "row", axis=3, tiled=True)
    return contract(tap_stack, gathered)


def per_device(radar_field, kernels, norm_gain_weights):
    tile_rows, tile_cols, channels = radar_field.shape
    dilation_list = [FIRST_DILATION, SECOND_DILATION]
    current = radar_field
    for block_index in range(BLOCKS):
        cast_state = current.astype(jnp.bfloat16)
        spacing = dilation_list[block_index]
        tap_stack = dilated_taps(cast_state, spacing // tile_rows, spacing // tile_cols)
        dilated_output = convolve(tap_stack, kernels, block_index, 0)
        mean_square = jnp.mean(dilated_output * dilated_output, axis=-1, keepdims=True)
        normed = (
            dilated_output / jnp.sqrt(mean_square + norm_floor) * norm_gain_weights[block_index]
        )
        hidden = jax.nn.relu(normed).astype(jnp.bfloat16).reshape(tile_rows, tile_cols, channels)
        padded = extended(hidden, (("row", 0), ("col", 1)), 1)
        plain_taps = []
        for row_off in range(3):
            for col_off in range(3):
                plain_taps.append(
                    padded[row_off : row_off + tile_rows, col_off : col_off + tile_cols]
                )
        plain = convolve(jnp.stack(plain_taps), kernels, block_index, 1)
        current = current + plain.reshape(tile_rows, tile_cols, channels)
    return current


def solution(mesh):
    return jax.shard_map(
        per_device,
        mesh=mesh,
        in_specs=(P("row", "col", None), P(None, None, None, None, None, "row"), P()),
        out_specs=P("row", "col", None),
        check_vma=False,
    )
```

profile of v0, /device:TPU:0, one launch (start us, length us, event | category | flops | bytes accessed | tf_op | source)
XLA Modules:
  0.0 160.9 jit_solution(17205378210213592081)
XLA Ops:
  6.5 0.0 copy-start
  6.5 0.0 copy-start.1
  6.5 0.0 all-gather.9.cloned.1.call-start
  6.5 2.5 %fusion.2 = (bf16[1,1,3,3,384,48]{4,5,3,2,1,0:T(8,128)(2,1)}, bf16[1,1,3,3,384,48]{4,5,3,2,1,0:T(8,128)(2,1)}, bf16[1,1,3,3,384,48]{4,5,3,2,1,0:T(8,128)(2,1)}, bf16[1,1,3,3,384,48]{4,5,3,2,1,0:T(8,128)(2,1)}) fusion(bf16[2,2,3,3,384,48]{4,5,3,2,1,0:T(8,128)(2,1)} %param.4), kind=kLoop, calls=%fused_computation.68 | loop fusion | bytes 2654208 | tf_op jit(solution)/shard_map/slice | solution.py:75
  9.0 0.0 all-gather.9.cloned.1.call-update
  9.0 0.0 all-gather.11.cloned.1.call-start
  9.1 0.7 all-gather.11.cloned.1.call-update
  9.8 0.0 all-gather.13.cloned.1.call-start
  9.8 0.0 copy-done
  9.9 6.0 %collective-permute-start = (bf16[8,16,384]{2,1,0:T(8,128)(2,1)S(1)}, bf16[8,16,384]{2,1,0:T(8,128)(2,1)S(1)}, u32[]{:S(2)}, u32[]{:S(2)}) collective-permute-start(bf16[8,16,384]{2,1,0:T(8,128)(2,1)S(1)} %convert_element_type.12), channel_id=1, source_target_pairs={{0,16},{4,20},{8,24},{12,28},{1,17},{5,21},{9,25},{13,29},{2,18},{... | collective-permute-start | bytes 294920 | tf_op jit(solution)/shard_map/ppermute | solution.py:17
  15.8 1.3 collective-permute-start.1
  17.2 0.9 collective-permute-done
  18.0 11.2 %collective-permute-done.1 = bf16[8,16,384]{2,1,0:T(8,128)(2,1)S(1)} collective-permute-done((bf16[8,16,384]{2,1,0:T(8,128)(2,1)S(1)}, bf16[8,16,384]{2,1,0:T(8,128)(2,1)S(1)}, u32[]{:S(2)}, u32[]{:S(2)}) %collective-permute-start.1) | collective-permute-done | bytes 98336 | tf_op jit(solution)/shard_map/ppermute | solution.py:17
  29.3 3.5 %collective-permute-start.2 = (bf16[3,8,16,384]{3,2,1,0:T(8,128)(2,1)S(1)}, bf16[3,8,16,384]{3,2,1,0:T(8,128)(2,1)S(1)}, u32[]{:S(2)}, u32[]{:S(2)}) collective-permute-start(bf16[3,8,16,384]{3,2,1,0:T(8,128)(2,1)S(1)} %pad_maximum_fusion), channel_id=1, source_target_pairs={{0,2},{1,3},{4,6},{5,7},{8,10},{9,11},{12,14},{13,15},{16,18},{17,... | collective-permute-start | bytes 884744 | tf_op jit(solution)/shard_map/ppermute | solution.py:17
  32.7 0.0 all-gather.13.cloned.1.call-update
  32.8 0.0 all-gather.15.cloned.1.call-start
  32.8 0.0 copy-done.1
  32.8 1.3 collective-permute-start.3
  34.1 2.8 %collective-permute-done.2 = bf16[3,8,16,384]{3,2,1,0:T(8,128)(2,1)S(1)} collective-permute-done((bf16[3,8,16,384]{3,2,1,0:T(8,128)(2,1)S(1)}, bf16[3,8,16,384]{3,2,1,0:T(8,128)(2,1)S(1)}, u32[]{:S(2)}, u32[]{:S(2)}) %collective-permute-start.2) | collective-permute-done | bytes 294944 | tf_op jit(solution)/shard_map/ppermute | solution.py:17
  37.0 4.4 %collective-permute-done.3 = bf16[3,8,16,384]{3,2,1,0:T(8,128)(2,1)S(1)} collective-permute-done((bf16[3,8,16,384]{3,2,1,0:T(8,128)(2,1)S(1)}, bf16[3,8,16,384]{3,2,1,0:T(8,128)(2,1)S(1)}, u32[]{:S(2)}, u32[]{:S(2)}) %collective-permute-start.3) | collective-permute-done | bytes 294944 | tf_op jit(solution)/shard_map/ppermute | solution.py:17
  41.7 6.2 %all-gather.9.cloned.1.call-done = bf16[1,1,3,3,384,384]{4,5,3,2,1,0:T(8,128)(2,1)} async-done(((bf16[1,1,3,3,384,48]{4,5,3,2,1,0:T(8,128)(2,1)}), bf16[1,1,3,3,384,384]{4,5,3,2,1,0:T(8,128)(2,1)}) %all-gather.9.cloned.1.call-update) | async-done | bytes 2654224 | tf_op jit(solution)/shard_map/all_gather | solution.py:75
  47.8 2.7 %multiply_reduce_fusion.1 = (f32[128]{0:T(128)S(1)}, f32[128,384]{1,0:T(8,128)S(1)}) fusion(bf16[9,128,384]{2,1,0:T(8,128)(2,1)S(1)} %constant_dynamic-update-slice_fusion, bf16[9,384,384]{1,2,0:T(8,128)(2,1)} %bitcast.139), kind=kOutput, calls=%fused_computation.11 | convolution fusion | flops 339836800 | bytes 3736064 | tf_op jit(solution)/shard_map/dot_general | solution.py:69
  50.6 0.1 maximum_convert_fusion.1
  50.7 2.1 %collective-permute-start.4 = (bf16[1,16,384]{2,1,0:T(8,128)(2,1)S(1)}, bf16[1,16,384]{2,1,0:T(8,128)(2,1)S(1)}, u32[]{:S(2)}, u32[]{:S(2)}) collective-permute-start(bf16[1,16,384]{2,1,0:T(8,128)(2,1)S(1)} %get-tuple-element.47), channel_id=1, source_target_pairs={{0,4},{4,8},{8,12},{12,16},{16,20},{20,24},{24,28},{1,5},{5,9},{9,... | collective-permute-start | bytes 36872 | tf_op jit(solution)/shard_map/ppermute | solution.py:28
  52.9 1.3 collective-permute-start.5
  54.2 0.0 collective-permute-done.4
  54.2 1.8 %collective-permute-done.5 = bf16[1,16,384]{2,1,0:T(8,128)(2,1)S(1)} collective-permute-done((bf16[1,16,384]{2,1,0:T(8,128)(2,1)S(1)}, bf16[1,16,384]{2,1,0:T(8,128)(2,1)S(1)}, u32[]{:S(2)}, u32[]{:S(2)}) %collective-permute-start.5) | collective-permute-done | bytes 12320 | tf_op jit(solution)/shard_map/ppermute | solution.py:30
  56.0 3.4 %collective-permute-start.6 = (bf16[10,1,384]{2,1,0:T(2,128)(2,1)S(1)}, bf16[10,1,384]{2,1,0:T(2,128)(2,1)S(1)}, u32[]{:S(2)}, u32[]{:S(2)}) collective-permute-start(bf16[10,1,384]{2,1,0:T(2,128)(2,1)S(1)} %get-tuple-element.40), channel_id=1, source_target_pairs={{0,1},{1,2},{2,3},{4,5},{5,6},{6,7},{8,9},{9,10},{10,11},{12,13},{... | collective-permute-start | bytes 23048 | tf_op jit(solution)/shard_map/ppermute | solution.py:28
  59.4 1.3 collective-permute-start.7
  60.7 0.1 collective-permute-done.6
  60.8 4.2 %collective-permute-done.7 = bf16[10,1,384]{2,1,0:T(2,128)(2,1)S(1)} collective-permute-done((bf16[10,1,384]{2,1,0:T(2,128)(2,1)S(1)}, bf16[10,1,384]{2,1,0:T(2,128)(2,1)S(1)}, u32[]{:S(2)}, u32[]{:S(2)}) %collective-permute-start.7) | collective-permute-done | bytes 7712 | tf_op jit(solution)/shard_map/ppermute | solution.py:30
  65.0 0.1 pad_maximum_fusion.2
  65.1 0.1 fusion.9
  65.2 0.1 bitcast_dynamic-update-slice_fusion.16
  65.5 16.2 %all-gather.11.cloned.1.call-done = bf16[1,1,3,3,384,384]{4,5,3,2,1,0:T(8,128)(2,1)} async-done(((bf16[1,1,3,3,384,48]{4,5,3,2,1,0:T(8,128)(2,1)}), bf16[1,1,3,3,384,384]{4,5,3,2,1,0:T(8,128)(2,1)}) %all-gather.11.cloned.1.call-update) | async-done | bytes 2654224 | tf_op jit(solution)/shard_map/all_gather | solution.py:75
  81.7 2.6 %fusion.11 = (bf16[8,16,384]{2,1,0:T(8,128)(2,1)S(1)}, f32[8,16,384]{2,1,0:T(8,128)S(1)}) fusion(f32[8,16,384]{2,1,0:T(8,128)S(1)} %copy-done, bf16[8,16,9,384]{3,1,0,2:T(8,128)(2,1)S(1)} %bitcast.147, bf16[9,384,384,1]{1,2,3,0:T(8,128)(2,1)} %bitcast.138), kind=kOutput, calls=%fused_computation.77 | convolution fusion | flops 339836928 | bytes 4030464 | tf_op jit(solution)/shard_map/dot_general | solution.py:69
  84.3 0.7 collective-permute-start.8
  85.0 0.0 all-gather.15.cloned.1.call-update
  85.0 0.0 collective-permute-done.8
  85.1 0.7 collective-permute-start.9
  85.8 0.0 collective-permute-done.9
  86.0 30.4 %all-gather.13.cloned.1.call-done = bf16[1,1,3,3,384,384]{4,5,3,2,1,0:T(8,128)(2,1)} async-done(((bf16[1,1,3,3,384,48]{4,5,3,2,1,0:T(8,128)(2,1)}), bf16[1,1,3,3,384,384]{4,5,3,2,1,0:T(8,128)(2,1)}) %all-gather.13.cloned.1.call-update) | async-done | bytes 2654224 | tf_op jit(solution)/shard_map/all_gather | solution.py:75
  116.4 2.8 %multiply_reduce_fusion = (f32[128]{0:T(128)S(1)}, f32[128,384]{1,0:T(8,128)S(1)}) fusion(bf16[9,128,384]{2,1,0:T(8,128)(2,1)S(1)} %constant_dynamic-update-slice_fusion.6, bf16[9,384,384]{1,2,0:T(8,128)(2,1)} %bitcast.137), kind=kOutput, calls=%fused_computation.9 | convolution fusion | flops 339836800 | bytes 3736064 | tf_op jit(solution)/shard_map/dot_general | solution.py:69
  119.2 0.1 maximum_convert_fusion
  119.3 2.1 %collective-permute-start.10 = (bf16[1,16,384]{2,1,0:T(8,128)(2,1)S(1)}, bf16[1,16,384]{2,1,0:T(8,128)(2,1)S(1)}, u32[]{:S(2)}, u32[]{:S(2)}) collective-permute-start(bf16[1,16,384]{2,1,0:T(8,128)(2,1)S(1)} %get-tuple-element.43), channel_id=1, source_target_pairs={{0,4},{4,8},{8,12},{12,16},{16,20},{20,24},{24,28},{1,5},{5,9},{9,... | collective-permute-start | bytes 36872 | tf_op jit(solution)/shard_map/ppermute | solution.py:28
  121.4 1.3 collective-permute-start.11
  122.7 0.0 collective-permute-done.10
  122.8 2.2 %collective-permute-done.11 = bf16[1,16,384]{2,1,0:T(8,128)(2,1)S(1)} collective-permute-done((bf16[1,16,384]{2,1,0:T(8,128)(2,1)S(1)}, bf16[1,16,384]{2,1,0:T(8,128)(2,1)S(1)}, u32[]{:S(2)}, u32[]{:S(2)}) %collective-permute-start.11) | collective-permute-done | bytes 12320 | tf_op jit(solution)/shard_map/ppermute | solution.py:30
  125.0 3.4 %collective-permute-start.12 = (bf16[10,1,384]{2,1,0:T(2,128)(2,1)S(1)}, bf16[10,1,384]{2,1,0:T(2,128)(2,1)S(1)}, u32[]{:S(2)}, u32[]{:S(2)}) collective-permute-start(bf16[10,1,384]{2,1,0:T(2,128)(2,1)S(1)} %get-tuple-element.36), channel_id=1, source_target_pairs={{0,1},{1,2},{2,3},{4,5},{5,6},{6,7},{8,9},{9,10},{10,11},{12,13},{... | collective-permute-start | bytes 23048 | tf_op jit(solution)/shard_map/ppermute | solution.py:28
  128.3 1.3 collective-permute-start.13
  129.7 0.1 collective-permute-done.12
  129.8 4.2 %collective-permute-done.13 = bf16[10,1,384]{2,1,0:T(2,128)(2,1)S(1)} collective-permute-done((bf16[10,1,384]{2,1,0:T(2,128)(2,1)S(1)}, bf16[10,1,384]{2,1,0:T(2,128)(2,1)S(1)}, u32[]{:S(2)}, u32[]{:S(2)}) %collective-permute-start.13) | collective-permute-done | bytes 7712 | tf_op jit(solution)/shard_map/ppermute | solution.py:30
  134.0 0.1 pad_maximum_fusion.3
  134.2 0.1 bitcast_dynamic-update-slice_fusion.4
  134.5 16.6 %all-gather.15.cloned.1.call-done = bf16[1,1,3,3,384,384]{4,5,3,2,1,0:T(8,128)(2,1)} async-done(((bf16[1,1,3,3,384,48]{4,5,3,2,1,0:T(8,128)(2,1)}), bf16[1,1,3,3,384,384]{4,5,3,2,1,0:T(8,128)(2,1)}) %all-gather.15.cloned.1.call-update) | async-done | bytes 2654224 | tf_op jit(solution)/shard_map/all_gather | solution.py:75
  151.0 3.3 %fusion.1 = f32[8,16,384]{2,1,0:T(8,128)} fusion(f32[8,16,384]{2,1,0:T(8,128)S(1)} %get-tuple-element.52, bf16[8,16,9,384]{3,1,0,2:T(8,128)(2,1)S(1)} %bitcast.148, bf16[9,384,384,1]{1,2,3,0:T(8,128)(2,1)} %bitcast.140), kind=kOutput, calls=%fused_computation.5 | convolution fusion | flops 339787776 | bytes 3932160 | tf_op jit(solution)/shard_map/dot_general | solution.py:69
  (51 shorter events, 1.1 us)
Async XLA Ops:
  6.5 3.3 %copy-start = (f32[8,16,384]{2,1,0:T(8,128)S(1)}, f32[8,16,384]{2,1,0:T(8,128)}, u32[]{:S(2)}) copy-start(f32[8,16,384]{2,1,0:T(8,128)} %param.3) | copy-start | bytes 589828
  6.5 26.3 %copy-start.1 = (f32[2,384]{1,0:T(2,128)S(1)}, f32[2,384]{1,0:T(2,128)}, u32[]{:S(2)}) copy-start(f32[2,384]{1,0:T(2,128)} %param.5) | copy-start | bytes 9220
  6.5 41.3 %all-gather.9.cloned.1.call-start = ((), (), s32[]{:S(2)}) async-start(), calls=%async_computation | async-start | bytes 2985984 | tf_op jit(solution)/shard_map/all_gather | solution.py:75
  9.0 72.6 %all-gather.11.cloned.1.call-start = ((), (), s32[]{:S(2)}) async-start(), calls=%async_computation.1 | async-start | bytes 2985984 | tf_op jit(solution)/shard_map/all_gather | solution.py:75
  9.8 106.6 %all-gather.13.cloned.1.call-start = ((), (), s32[]{:S(2)}) async-start(), calls=%async_computation.2 | async-start | bytes 2985984 | tf_op jit(solution)/shard_map/all_gather | solution.py:75
  9.9 8.2 %collective-permute-start = (bf16[8,16,384]{2,1,0:T(8,128)(2,1)S(1)}, bf16[8,16,384]{2,1,0:T(8,128)(2,1)S(1)}, u32[]{:S(2)}, u32[]{:S(2)}) collective-permute-start(bf16[8,16,384]{2,1,0:T(8,128)(2,1)S(1)} %convert_element_type.12), channel_id=1, source_target_pairs={{0,16},{4,20},{8,24},{12,28},{1,17},{5,21},{9,25},{13,29},{2,18},{... | collective-permute-start | bytes 294920 | tf_op jit(solution)/shard_map/ppermute | solution.py:17
  15.8 13.4 %collective-permute-start.1 = (bf16[8,16,384]{2,1,0:T(8,128)(2,1)S(1)}, bf16[8,16,384]{2,1,0:T(8,128)(2,1)S(1)}, u32[]{:S(2)}, u32[]{:S(2)}) collective-permute-start(bf16[8,16,384]{2,1,0:T(8,128)(2,1)S(1)} %convert_element_type.12), channel_id=1, source_target_pairs={{16,0},{20,4},{24,8},{28,12},{17,1},{21,5},{25,9},{29,13},{18,2},{... | collective-permute-start | bytes 294920 | tf_op jit(solution)/shard_map/ppermute | solution.py:17
  29.3 7.7 %collective-permute-start.2 = (bf16[3,8,16,384]{3,2,1,0:T(8,128)(2,1)S(1)}, bf16[3,8,16,384]{3,2,1,0:T(8,128)(2,1)S(1)}, u32[]{:S(2)}, u32[]{:S(2)}) collective-permute-start(bf16[3,8,16,384]{3,2,1,0:T(8,128)(2,1)S(1)} %pad_maximum_fusion), channel_id=1, source_target_pairs={{0,2},{1,3},{4,6},{5,7},{8,10},{9,11},{12,14},{13,15},{16,18},{17,... | collective-permute-start | bytes 884744 | tf_op jit(solution)/shard_map/ppermute | solution.py:17
  32.8 118.2 %all-gather.15.cloned.1.call-start = ((), (), s32[]{:S(2)}) async-start(), calls=%async_computation.3 | async-start | bytes 2985984 | tf_op jit(solution)/shard_map/all_gather | solution.py:75
  32.8 8.6 %collective-permute-start.3 = (bf16[3,8,16,384]{3,2,1,0:T(8,128)(2,1)S(1)}, bf16[3,8,16,384]{3,2,1,0:T(8,128)(2,1)S(1)}, u32[]{:S(2)}, u32[]{:S(2)}) collective-permute-start(bf16[3,8,16,384]{3,2,1,0:T(8,128)(2,1)S(1)} %pad_maximum_fusion), channel_id=1, source_target_pairs={{2,0},{3,1},{6,4},{7,5},{10,8},{11,9},{14,12},{15,13},{18,16},{19,... | collective-permute-start | bytes 884744 | tf_op jit(solution)/shard_map/ppermute | solution.py:17
  50.7 3.4 %collective-permute-start.4 = (bf16[1,16,384]{2,1,0:T(8,128)(2,1)S(1)}, bf16[1,16,384]{2,1,0:T(8,128)(2,1)S(1)}, u32[]{:S(2)}, u32[]{:S(2)}) collective-permute-start(bf16[1,16,384]{2,1,0:T(8,128)(2,1)S(1)} %get-tuple-element.47), channel_id=1, source_target_pairs={{0,4},{4,8},{8,12},{12,16},{16,20},{20,24},{24,28},{1,5},{5,9},{9,... | collective-permute-start | bytes 36872 | tf_op jit(solution)/shard_map/ppermute | solution.py:28
  52.9 3.1 %collective-permute-start.5 = (bf16[1,16,384]{2,1,0:T(8,128)(2,1)S(1)}, bf16[1,16,384]{2,1,0:T(8,128)(2,1)S(1)}, u32[]{:S(2)}, u32[]{:S(2)}) collective-permute-start(bf16[1,16,384]{2,1,0:T(8,128)(2,1)S(1)} %get-tuple-element.48), channel_id=1, source_target_pairs={{4,0},{8,4},{12,8},{16,12},{20,16},{24,20},{28,24},{5,1},{9,5},{13... | collective-permute-start | bytes 36872 | tf_op jit(solution)/shard_map/ppermute | solution.py:30
  56.0 4.8 %collective-permute-start.6 = (bf16[10,1,384]{2,1,0:T(2,128)(2,1)S(1)}, bf16[10,1,384]{2,1,0:T(2,128)(2,1)S(1)}, u32[]{:S(2)}, u32[]{:S(2)}) collective-permute-start(bf16[10,1,384]{2,1,0:T(2,128)(2,1)S(1)} %get-tuple-element.40), channel_id=1, source_target_pairs={{0,1},{1,2},{2,3},{4,5},{5,6},{6,7},{8,9},{9,10},{10,11},{12,13},{... | collective-permute-start | bytes 23048 | tf_op jit(solution)/shard_map/ppermute | solution.py:28
  59.4 5.6 %collective-permute-start.7 = (bf16[10,1,384]{2,1,0:T(2,128)(2,1)S(1)}, bf16[10,1,384]{2,1,0:T(2,128)(2,1)S(1)}, u32[]{:S(2)}, u32[]{:S(2)}) collective-permute-start(bf16[10,1,384]{2,1,0:T(2,128)(2,1)S(1)} %get-tuple-element.39), channel_id=1, source_target_pairs={{1,0},{2,1},{3,2},{5,4},{6,5},{7,6},{9,8},{10,9},{11,10},{13,12},{... | collective-permute-start | bytes 23048 | tf_op jit(solution)/shard_map/ppermute | solution.py:30
  84.3 0.7 collective-permute-start.8
  85.1 0.7 collective-permute-start.9
  119.3 3.4 %collective-permute-start.10 = (bf16[1,16,384]{2,1,0:T(8,128)(2,1)S(1)}, bf16[1,16,384]{2,1,0:T(8,128)(2,1)S(1)}, u32[]{:S(2)}, u32[]{:S(2)}) collective-permute-start(bf16[1,16,384]{2,1,0:T(8,128)(2,1)S(1)} %get-tuple-element.43), channel_id=1, source_target_pairs={{0,4},{4,8},{8,12},{12,16},{16,20},{20,24},{24,28},{1,5},{5,9},{9,... | collective-permute-start | bytes 36872 | tf_op jit(solution)/shard_map/ppermute | solution.py:28
  121.4 3.5 %collective-permute-start.11 = (bf16[1,16,384]{2,1,0:T(8,128)(2,1)S(1)}, bf16[1,16,384]{2,1,0:T(8,128)(2,1)S(1)}, u32[]{:S(2)}, u32[]{:S(2)}) collective-permute-start(bf16[1,16,384]{2,1,0:T(8,128)(2,1)S(1)} %get-tuple-element.44), channel_id=1, source_target_pairs={{4,0},{8,4},{12,8},{16,12},{20,16},{24,20},{28,24},{5,1},{9,5},{13... | collective-permute-start | bytes 36872 | tf_op jit(solution)/shard_map/ppermute | solution.py:30
  125.0 4.8 %collective-permute-start.12 = (bf16[10,1,384]{2,1,0:T(2,128)(2,1)S(1)}, bf16[10,1,384]{2,1,0:T(2,128)(2,1)S(1)}, u32[]{:S(2)}, u32[]{:S(2)}) collective-permute-start(bf16[10,1,384]{2,1,0:T(2,128)(2,1)S(1)} %get-tuple-element.36), channel_id=1, source_target_pairs={{0,1},{1,2},{2,3},{4,5},{5,6},{6,7},{8,9},{9,10},{10,11},{12,13},{... | collective-permute-start | bytes 23048 | tf_op jit(solution)/shard_map/ppermute | solution.py:28
  128.3 5.6 %collective-permute-start.13 = (bf16[10,1,384]{2,1,0:T(2,128)(2,1)S(1)}, bf16[10,1,384]{2,1,0:T(2,128)(2,1)S(1)}, u32[]{:S(2)}, u32[]{:S(2)}) collective-permute-start(bf16[10,1,384]{2,1,0:T(2,128)(2,1)S(1)} %get-tuple-element.35), channel_id=1, source_target_pairs={{1,0},{2,1},{3,2},{5,4},{6,5},{7,6},{9,8},{10,9},{11,10},{13,12},{... | collective-permute-start | bytes 23048 | tf_op jit(solution)/shard_map/ppermute | solution.py:30
Sparse Core Ops, SparseCore 0:
  9.1 38.6 all-gather.8
  49.4 32.1 all-gather.10
  83.3 33.0 all-gather.12
  117.9 33.0 all-gather.14
where the time goes:
time: 161 us
  waiting for transfers between devices  102 us (63%)
  starting transfers between devices  29.7 us (18%)
  between operations  13.7 us (9%)
  matrix products  11.5 us (7%)
  local copies, waits for them, and re-layouts  3.35 us (2%)
    all_gather x4, waiting for transfers between devices, convolve(): lax.all_gather(kernels[block_index, which], 'row', axis=3, tiled=True)  69.3 us
    ppermute x6, waiting for transfers between devices, passed_along(): lax.ppermute(value, axis, [(source, source + steps) for source in range(i...  19.3 us
    ppermute x6, starting transfers between devices, passed_along(): lax.ppermute(value, axis, [(source, source + steps) for source in range(i...  13.4 us
    ppermute x4, waiting for transfers between devices, extended(): lax.ppermute(head, axis, [((i + 1) % count, i) for i in range(ends)])  12.3 us
    dot_general x4, matrix products, contract(): lax.dot_general(flat_taps, flat_kernel, (((0, 2), (0, 1)), ((), ())), pre...  11.5 us
    ppermute x4, starting transfers between devices, extended(): lax.ppermute(tail, axis, [(i, (i + 1) % count) for i in range(ends)])  11 us
    ppermute x4, starting transfers between devices, extended(): lax.ppermute(head, axis, [((i + 1) % count, i) for i in range(ends)])  5.17 us
  transfers between devices with their start and end apart: 18, of which 14 were waited for; matrix products, arithmetic and copies ran while one was open for 6% of the time, Pallas kernels for 0%

commit v1 on v0

--- a/solution.py
+++ b/solution.py
@@ -1,6 +1,10 @@
+import functools
+
 import jax
 import jax.numpy as jnp
 from jax import lax
+from jax.experimental import pallas as pl
+from jax.experimental.pallas import tpu as pltpu
 from jax.sharding import PartitionSpec as P
 
 BLOCKS = 2
@@ -102,9 +106,375 @@
     return current
 
 
+MESH = pl.DeviceIdType.MESH
+PLANE = 4
+
+
+def fits(rows, cols, tile, shard):
+    height, width = rows * tile[0], cols * tile[1]
+    return (
+        cols == PLANE
+        and rows % 4 == 0
+        and height == 2 * FIRST_DILATION
+        and width == 2 * FIRST_DILATION
+        and SECOND_DILATION >= max(height, width)
+        and shard[-1] % 16 == 0
+        and tile[1] % 16 == 0
+    )
+
+
+def block_kernel(
+    rows, cols, th, tw, taps,
+    x_ref, w_ref, radar_ref, gain_ref, o_ref,
+    wg, xin, hs, ce, rowhalo, colhalo, hp, current,
+    local_sem, w_recv, up_send, down_send, x_send, y_send, diag_send, core_send, core_recv,
+    tile_send, tile_recv, halo_send, halo_recv,
+):
+    row, col = lax.axis_index("row"), lax.axis_index("col")
+    depth = rows // 2
+    groups = taps // cols
+    z, core = row // 2, row % 2
+    channels = x_ref.shape[-1]
+    col_of = [col, col + 1 - 2 * (col % 2), (col + 2) % 4, 3 - col]
+    other_core = row + 1 - 2 * core
+    far_row = (row + depth) % rows
+    far_col = col_of[2]
+
+    def remote(source, target, send, recv, to_row, to_col):
+        return pltpu.make_async_remote_copy(
+            src_ref=source,
+            dst_ref=target,
+            send_sem=send,
+            recv_sem=recv,
+            device_id={"row": to_row, "col": to_col},
+            device_id_type=MESH,
+        )
+
+    for g in range(groups):
+        span = pl.ds(g * cols, cols)
+        pltpu.make_async_copy(w_ref.at[span], wg.at[span, z, core], local_sem.at[g]).start()
+
+    neighbours = []
+    for dr in (-1, 0, 1):
+        for dc in (-1, 0, 1):
+            if dr or dc:
+                ok = (row + dr >= 0) & (row + dr < rows) & (col + dc >= 0) & (col + dc < cols)
+                neighbours.append((dr, dc, ok))
+
+    barrier = pltpu.get_barrier_semaphore()
+    greeted = [
+        (z > 0, row - 2, col),
+        (z < depth - 1, row + 2, col),
+        (None, row, col_of[1]),
+        (None, row, col_of[2]),
+        (None, other_core, col),
+        (None, far_row, col),
+    ] + [(ok, row + dr, col + dc) for dr, dc, ok in neighbours]
+    expected = 0
+    for ok, to_row, to_col in greeted:
+        def greet(to_row=to_row, to_col=to_col):
+            pl.semaphore_signal(barrier, inc=1, device_id={"row": to_row, "col": to_col}, device_id_type=MESH)
+
+        if ok is None:
+            greet()
+            expected = expected + 1
+        else:
+            pl.when(ok)(greet)
+            expected = expected + jnp.where(ok, 1, 0)
+    hp[...] = jnp.zeros_like(hp)
+    for g in range(groups):
+        span = pl.ds(g * cols, cols)
+        pltpu.make_async_copy(w_ref.at[span], wg.at[span, z, core], local_sem.at[g]).wait()
+    pl.semaphore_wait(barrier, expected)
+
+    def piece(g, j, source):
+        return wg.at[cols * g + col_of[j], source, core]
+
+    def z_up(g, source):
+        p = piece(g, 0, source)
+        return remote(p, p, up_send.at[g, source], w_recv.at[g, 0, source], row + 2, col)
+
+    def z_down(g, source):
+        p = piece(g, 0, source)
+        return remote(p, p, down_send.at[g, source], w_recv.at[g, 0, source], row - 2, col)
+
+    def to_x(g, source):
+        p = piece(g, 0, source)
+        return remote(p, p, x_send.at[g, source], w_recv.at[g, 1, source], row, col_of[1])
+
+    def to_y(g, source):
+        p = piece(g, 0, source)
+        return remote(p, p, y_send.at[g, source], w_recv.at[g, 2, source], row, col_of[2])
+
+    def relay_via(g):
+        return 1 if g % 3 == 0 else 2
+
+    def to_diag(g, source):
+        via = relay_via(g)
+        p = piece(g, via, source)
+        return remote(p, p, diag_send.at[g, source], w_recv.at[g, 3, source], row, col_of[3 - via])
+
+    def to_core(g, j):
+        p = wg.at[cols * g + col_of[j], :, core]
+        return remote(p, p, core_send.at[g, j], core_recv.at[g, j], other_core, col)
+
+    def from_core(g, j):
+        p = wg.at[cols * g + col_of[j], :, 1 - core]
+        return remote(p, p, core_send.at[g, j], core_recv.at[g, j], other_core, col)
+
+    def arrived(g, j, source):
+        p = piece(g, j, source)
+        remote(p, p, x_send.at[g, source], w_recv.at[g, j, source], row, col_of[1]).wait_recv()
+
+    def others(act):
+        for d in range(1, depth):
+            for side in (-1, 1):
+                source = z + side * d
+                pl.when((source >= 0) & (source < depth))(functools.partial(act, source, side, d))
+
+    def own_z(g):
+        pl.when(z < depth - 1)(lambda: z_up(g, z).start())
+        pl.when(z > 0)(lambda: z_down(g, z).start())
+
+    def z_phase(g):
+        def act(source, side, d):
+            arrived(g, 0, source)
+            if side < 0:
+                pl.when(z < depth - 1)(lambda: z_up(g, source).start())
+            else:
+                pl.when(z > 0)(lambda: z_down(g, source).start())
+            to_x(g, source).start()
+            to_y(g, source).start()
+
+        others(act)
+        to_core(g, 0).start()
+
+    def plane_phase(g):
+        via = relay_via(g)
+
+        def act(source, side, d):
+            arrived(g, via, source)
+            to_diag(g, source).start()
+            arrived(g, 3 - via, source)
+
+        others(act)
+        to_core(g, 1).start()
+        to_core(g, 2).start()
+
+    def diag_phase(g):
+        others(lambda source, side, d: arrived(g, 3, source))
+        to_core(g, 3).start()
+
+    def core_phase(g):
+        for j in range(4):
+            from_core(g, j).wait_recv()
+
+    tile_copies = [
+        remote(x_ref, xin.at[0], tile_send.at[0], tile_recv.at[0], far_row, col),
+        remote(x_ref, xin.at[1], tile_send.at[1], tile_recv.at[1], row, far_col),
+        remote(xin.at[0], xin.at[2], tile_send.at[2], tile_recv.at[2], row, far_col),
+    ]
+
+    def product(cells, tap):
+        weight = wg[tap].reshape(channels, channels)
+        return lax.dot_general(cells, weight, (((1,), (1,)), ((), ())), preferred_element_type=jnp.float32)
+
+    def halo_copy(b, n):
+        dr, dc, _ = neighbours[n]
+        if dc == 0:
+            source = hs.at[b, 0 if dr < 0 else th - 1]
+            target = rowhalo.at[b, 1 if dr < 0 else 0]
+        else:
+            source = ce.at[b, 0 if dc < 0 else 1]
+            target = colhalo.at[b, 1 if dc < 0 else 0, 1 - dr]
+        return remote(source, target, halo_send.at[b, n], halo_recv.at[b, 7 - n], row + dr, col + dc)
+
+    def halo_arrived(b, n):
+        dr, dc, _ = neighbours[n]
+        if dc == 0:
+            target = rowhalo.at[b, 0 if dr < 0 else 1]
+        else:
+            target = colhalo.at[b, 0 if dc < 0 else 1, dr + 1]
+        remote(target, target, halo_send.at[b, n], halo_recv.at[b, n], row + dr, col + dc).wait_recv()
+
+    def normalize(b, dilated):
+        mean_square = jnp.mean(dilated * dilated, axis=-1, keepdims=True)
+        normed = dilated / jnp.sqrt(mean_square + norm_floor) * gain_ref[b : b + 1, :]
+        hidden = jax.nn.relu(normed).astype(jnp.bfloat16).reshape(th, tw, channels)
+        hs[b] = hidden
+        wide = hidden.astype(jnp.float32)
+        ce[b, 0] = wide[:, 0, :].astype(jnp.bfloat16)
+        ce[b, 1] = wide[:, tw - 1, :].astype(jnp.bfloat16)
+        hp[1 : th + 1, 1 : tw + 1, :] = wide
+        for n, (dr, dc, ok) in enumerate(neighbours):
+            pl.when(ok)(lambda n=n: halo_copy(b, n).start())
+
+    def take_halo(b):
+        for n, (dr, dc, ok) in enumerate(neighbours):
+            def act(n=n, dr=dr, dc=dc):
+                halo_arrived(b, n)
+                to_row = 0 if dr < 0 else th + 1
+                to_col = 0 if dc < 0 else tw + 1
+                if dc == 0:
+                    hp[to_row, 1 : tw + 1, :] = rowhalo[b, 0 if dr < 0 else 1].astype(jnp.float32)
+                else:
+                    edge = colhalo[b, 0 if dc < 0 else 1, dr + 1].astype(jnp.float32)
+                    if dr == 0:
+                        hp[1 : th + 1, to_col : to_col + 1, :] = edge.reshape(th, 1, channels)
+                    else:
+                        at = th - 1 if dr < 0 else 0
+                        hp[to_row, to_col : to_col + 1, :] = edge[at : at + 1, :]
+
+            pl.when(ok)(act)
+
+    def shifted(tap):
+        p, q = tap // 3, tap % 3
+        return hp[p : p + th, q : q + tw, :].astype(jnp.bfloat16).reshape(th * tw, channels)
+
+    def first_block():
+        tile_copies[1].wait_recv()
+        tile_copies[2].wait_recv()
+        far_p = jnp.where(row < depth, 2, 0)
+        far_q = jnp.where(col < cols // 2, 2, 0)
+        dilated = product(x_ref[...], 4)
+        dilated += product(xin[0], far_p * 3 + 1)
+        dilated += product(xin[1], 3 + far_q)
+        dilated += product(xin[2], far_p * 3 + far_q)
+        normalize(0, dilated)
+
+    def plain(initial, last, base):
+        total = product(shifted(initial), base + initial)
+        for tap in range(initial + 1, last):
+            total += product(shifted(tap), base + tap)
+        return total
+
+    hooks = {}
+    first_plain, centre, second_plain = 9, 18, 19
+
+    tile_copies[0].start()
+    tile_copies[1].start()
+    own_z(0)
+    own_z(1)
+    ready = 0
+    stage = 0
+    for step in range(groups + 3):
+        if step < groups:
+            z_phase(step)
+            if step + 2 < groups:
+                own_z(step + 2)
+        if step == 1:
+            tile_copies[0].wait_recv()
+            tile_copies[2].start()
+        if 0 <= step - 1 < groups:
+            plane_phase(step - 1)
+        if 0 <= step - 2 < groups:
+            diag_phase(step - 2)
+        if step - 3 < 0:
+            continue
+        core_phase(step - 3)
+        ready = (step - 2) * cols
+        if stage == 0 and ready >= first_plain:
+            first_block()
+            stage = 1
+        elif stage == 1:
+            split = min(ready, centre) - first_plain
+            take_halo(0)
+            current[...] = radar_ref[...] + plain(0, split, first_plain)
+            done = split
+            stage = 2
+        if stage == 2 and ready > centre:
+            current[...] += plain(done, 9, first_plain)
+            normalize(1, product(current[...].astype(jnp.bfloat16), centre))
+            stage = 3
+        elif stage == 3:
+            split = min(ready, taps) - second_plain
+            take_halo(1)
+            current[...] += plain(0, split, second_plain)
+            done = split
+            stage = 4
+        elif stage == 4:
+            o_ref[...] = current[...] + plain(done, 9, second_plain)
+            stage = 5
+
+    for copy in tile_copies:
+        copy.wait_send()
+    for g in range(groups):
+        pl.when(z < depth - 1)(lambda: z_up(g, z).wait_send())
+        pl.when(z > 0)(lambda: z_down(g, z).wait_send())
+
+        def act(source, side, d):
+            if side < 0:
+                pl.when(z < depth - 1)(lambda: z_up(g, source).wait_send())
+            else:
+                pl.when(z > 0)(lambda: z_down(g, source).wait_send())
+            to_x(g, source).wait_send()
+            to_y(g, source).wait_send()
+            to_diag(g, source).wait_send()
+
+        others(act)
+        for j in range(4):
+            to_core(g, j).wait_send()
+    for b in range(2):
+        for n, (dr, dc, ok) in enumerate(neighbours):
+            pl.when(ok)(lambda: halo_copy(b, n).wait_send())
+
+
+def one_kernel(rows, cols, radar_field, kernels, norm_gain_weights):
+    th, tw, channels = radar_field.shape
+    part = kernels.shape[-1]
+    depth = rows // 2
+    flat = jnp.swapaxes(kernels.reshape(BLOCKS * 2, 9, channels, part), 2, 3)
+    weights = jnp.concatenate([flat[0], flat[1], flat[2, 4:5], flat[3]])
+    taps = weights.shape[0]
+    groups = taps // cols
+    flat_radar = radar_field.reshape(th * tw, channels)
+    vmem = pl.BlockSpec(memory_space=pltpu.VMEM)
+    dma = pltpu.SemaphoreType.DMA
+    out = pl.pallas_call(
+        functools.partial(block_kernel, rows, cols, th, tw, taps),
+        out_shape=jax.ShapeDtypeStruct((th * tw, channels), jnp.float32),
+        in_specs=[vmem, pl.BlockSpec(memory_space=pl.ANY), vmem, vmem],
+        out_specs=vmem,
+        scratch_shapes=[
+            pltpu.VMEM((taps, depth, 2, part, channels), jnp.bfloat16),
+            pltpu.VMEM((3, th * tw, channels), jnp.bfloat16),
+            pltpu.VMEM((2, th, tw, channels), jnp.bfloat16),
+            pltpu.VMEM((2, 2, th, channels), jnp.bfloat16),
+            pltpu.VMEM((2, 2, tw, channels), jnp.bfloat16),
+            pltpu.VMEM((2, 2, 3, th, channels), jnp.bfloat16),
+            pltpu.VMEM((th + 2, -(-(tw + 2) // 8) * 8, channels), jnp.float32),
+            pltpu.VMEM((th * tw, channels), jnp.float32),
+            dma((groups,)),
+            dma((groups, 4, depth)),
+            dma((groups, depth)),
+            dma((groups, depth)),
+            dma((groups, depth)),
+            dma((groups, depth)),
+            dma((groups, depth)),
+            dma((groups, 4)),
+            dma((groups, 4)),
+            dma((3,)),
+            dma((3,)),
+            dma((2, 8)),
+            dma((2, 8)),
+        ],
+        compiler_params=pltpu.CompilerParams(
+            collective_id=0, has_side_effects=True, vmem_limit_bytes=48 * 1024 * 1024
+        ),
+    )(flat_radar.astype(jnp.bfloat16), weights, flat_radar, norm_gain_weights)
+    return out.reshape(th, tw, channels)
+
+
 def solution(mesh):
+    rows, cols = mesh.shape["row"], mesh.shape["col"]
+
+    def body(radar_field, kernels, norm_gain_weights):
+        if fits(rows, cols, radar_field.shape, kernels.shape):
+            return one_kernel(rows, cols, radar_field, kernels, norm_gain_weights)
+        return per_device(radar_field, kernels, norm_gain_weights)
+
     return jax.shard_map(
-        per_device,
+        body,
         mesh=mesh,
         in_specs=(P("row", "col", None), P(None, None, None, None, None, "row"), P()),
         out_specs=P("row", "col", None),

time: 161 us -> 61.3 us (0.38)
  waiting for transfers between devices: 102 us -> 0 us
  Pallas kernels: 0 us -> 58.1 us
  starting transfers between devices: 29.7 us -> 0 us
  between operations: 13.7 us -> 0.05 us
  matrix products: 11.5 us -> 0 us
    all_gather x4 -> x0, waiting for transfers between devices: 69.3 us -> none  [convolve(): lax.all_gather(kernels[block_index, which], 'row', axis=3, tiled=True)]
    pallas_call x0 -> x1, Pallas kernels: none -> 58.1 us  [one_kernel(): pl.pallas_call(functools.partial(block_kernel, rows, cols, th, tw, taps),...]
    ppermute x14 -> x0, waiting for transfers between devices: 31.8 us -> none  [the longest x6 19.3 us: passed_along(): lax.ppermute(value, axis, [(source, source + steps) for source in range(i...]
    ppermute x14 -> x0, starting transfers between devices: 29.6 us -> none  [the longest x6 13.4 us: passed_along(): lax.ppermute(value, axis, [(source, source + steps) for source in range(i...]
    dot_general x4 -> x0, matrix products: 11.5 us -> none  [contract(): lax.dot_general(flat_taps, flat_kernel, (((0, 2), (0, 1)), ((), ())), pre...]
    slice x11 -> x0, local copies, waits for them, and re-layouts: 2.74 us -> none  [the longest x1 2.46 us: convolve(): kernels[block_index, which]]
    squeeze x0 -> x2, local copies, waits for them, and re-layouts: none -> 2.09 us  [one_kernel(): weights = jnp.concatenate([flat[0], flat[1], flat[2, 4:5], flat[3]])]
  transfers between devices with their start and end apart: 18 -> 0, of which waited for: 14 -> 0; matrix products, arithmetic and copies ran while one was open for 6% -> 0% of each run, Pallas kernels for 0% -> 0%
where the time goes in v1:
time: 61.3 us; the launch traced here: 61.1 us
  Pallas kernels  58.1 us (95%)
  local copies, waits for them, and re-layouts  2.78 us (5%)
    pallas_call x1, Pallas kernels, one_kernel(): pl.pallas_call(functools.partial(block_kernel, rows, cols, th, tw, taps),...  58.1 us
    squeeze x2, local copies, waits for them, and re-layouts, one_kernel(): weights = jnp.concatenate([flat[0], flat[1], flat[2, 4:5], flat[3]])  2.09 us

profile of v1, /device:TPU:0, one launch (start us, length us, event | category | flops | bytes accessed | tf_op | source)
XLA Modules:
  0.0 61.1 jit_solution(11384293670216638422)
XLA Ops:
  0.0 1.3 %slice_bitcast_fusion.2 = (bf16[9,48,384]{2,1,0:T(8,128)(2,1)S(1)}, bf16[9,48,384]{2,1,0:T(8,128)(2,1)S(1)}, bf16[9,48,384]{2,1,0:T(8,128)(2,1)S(1)}) fusion(bf16[4,9,48,384]{3,2,1,0:T(8,128)(2,1)} %bitcast.16), kind=kLoop, calls=%fused_computation.3 | loop fusion | bytes 1990656 | tf_op jit(solution)/shard_map/squeeze | solution.py:427
  1.3 0.0 copy-start
  1.3 0.0 copy-start.1
  1.3 0.8 %slice_bitcast_fusion.3 = bf16[1,48,384]{2,1,0:T(8,128)(2,1)S(1)} fusion(bf16[4,9,48,384]{3,2,1,0:T(8,128)(2,1)} %bitcast.17), kind=kLoop, calls=%fused_computation.4 | loop fusion | bytes 73728 | tf_op jit(solution)/shard_map/squeeze | solution.py:427
  2.1 0.2 pad_maximum_fusion.w_ref
  2.3 0.0 copy-done
  2.3 0.0 copy-done.1
  2.3 58.1 %shard_map.37 = f32[128,384]{1,0:T(8,128)S(1)} custom-call(bf16[128,384]{1,0:T(8,128)(2,1)S(1)} %bitcast_convert_fusion.x_ref, bf16[28,48,384]{2,1,0:T(8,128)(2,1)S(1)} %pad_maximum_fusion.w_ref, f32[128,384]{1,0:T(8,128)S(1)} %bitcast.14, f32[2,384]{1,0:T(2,128)S(1)} %copy-done.1), custom_call_target="tpu_custom_call" | custom-call | tf_op jit(solution)/shard_map/pallas_call | solution.py:433
  60.5 0.7 %copy.5 = f32[8,16,384]{2,1,0:T(8,128)} copy(f32[8,16,384]{2,1,0:T(8,128)S(1)} %bitcast.15) | data formatting | bytes 393216
  (1 shorter events, 0.0 us)
Async XLA Ops:
  1.3 1.0 %copy-start = (f32[8,16,384]{2,1,0:T(8,128)S(1)}, f32[8,16,384]{2,1,0:T(8,128)}, u32[]{:S(2)}) copy-start(f32[8,16,384]{2,1,0:T(8,128)} %param.3) | copy-start | bytes 589828
  1.3 1.0 %copy-start.1 = (f32[2,384]{1,0:T(2,128)S(1)}, f32[2,384]{1,0:T(2,128)}, u32[]{:S(2)}) copy-start(f32[2,384]{1,0:T(2,128)} %gain_ref.1) | copy-start | bytes 9220

commit v2 on v1

--- a/solution.py
+++ b/solution.py
@@ -108,6 +108,8 @@
 
 MESH = pl.DeviceIdType.MESH
 PLANE = 4
+AHEAD, Z_LAG, PLANE_LAG, DIAG_LAG, CORE_LAG = 3, 2, 2, 2, 2
+LONG_START, TILE_STEP = 4, 2
 
 
 def fits(rows, cols, tile, shard):
@@ -124,17 +126,18 @@
 
 
 def block_kernel(
-    rows, cols, th, tw, taps,
-    x_ref, w_ref, radar_ref, gain_ref, o_ref,
-    wg, xin, hs, ce, rowhalo, colhalo, hp, current,
-    local_sem, w_recv, up_send, down_send, x_send, y_send, diag_send, core_send, core_recv,
+    rows, cols, th, tw, taps, parts,
+    w_ref, radar_hbm, gain_hbm, o_ref,
+    wg, x_ref, gain_ref, xin, hs, ce, rowhalo, colhalo, hp, current,
+    load_sem,    local_sem, w_recv, up_send, down_send, x_send, y_send, diag_send, core_send, core_recv, own_send, own_recv,
     tile_send, tile_recv, halo_send, halo_recv,
 ):
     row, col = lax.axis_index("row"), lax.axis_index("col")
     depth = rows // 2
     groups = taps // cols
     z, core = row // 2, row % 2
-    channels = x_ref.shape[-1]
+    channels = o_ref.shape[-1]
+    half = depth // 2
     col_of = [col, col + 1 - 2 * (col % 2), (col + 2) % 4, 3 - col]
     other_core = row + 1 - 2 * core
     far_row = (row + depth) % rows
@@ -150,9 +153,19 @@
             device_id_type=MESH,
         )
 
-    for g in range(groups):
-        span = pl.ds(g * cols, cols)
-        pltpu.make_async_copy(w_ref.at[span], wg.at[span, z, core], local_sem.at[g]).start()
+    radar_copy = pltpu.make_async_copy(radar_hbm, current, load_sem.at[0])
+    gain_copy = pltpu.make_async_copy(gain_hbm, gain_ref, load_sem.at[1])
+    radar_copy.start()
+    gain_copy.start()
+    local_copies = []
+    filled = 0
+    for n, (conv, first, count) in enumerate(parts):
+        source = w_ref.at[conv, pl.ds(first, count)]
+        local_copies.append(
+            pltpu.make_async_copy(source, wg.at[pl.ds(filled, count), z, core], local_sem.at[n])
+        )
+        local_copies[-1].start()
+        filled += count
 
     neighbours = []
     for dr in (-1, 0, 1):
@@ -182,13 +195,62 @@
             pl.when(ok)(greet)
             expected = expected + jnp.where(ok, 1, 0)
     hp[...] = jnp.zeros_like(hp)
-    for g in range(groups):
-        span = pl.ds(g * cols, cols)
-        pltpu.make_async_copy(w_ref.at[span], wg.at[span, z, core], local_sem.at[g]).wait()
+    radar_copy.wait()
+    x_ref[...] = current[...].astype(jnp.bfloat16)
+    gain_copy.wait()
+    for copy in local_copies:
+        copy.wait()
     pl.semaphore_wait(barrier, expected)
 
-    def piece(g, j, source):
-        return wg.at[cols * g + col_of[j], source, core]
+    def along_z(g):
+        return g == groups - 1
+
+    def tap_of(g, j):
+        return cols * g + col_of[j]
+
+    def piece(g, j, source, of=None):
+        of = core if of is None else of
+        if along_z(g):
+            return wg.at[pl.ds(cols * g, cols), source, of]
+        return wg.at[tap_of(g, j), source, of]
+
+    def upper_only(g, j):
+        return tap_of(g, j) < 3
+
+    def lower_only(g, j):
+        return (tap_of(g, j) >= 6) & (tap_of(g, j) < 9)
+
+    def guarded(g, condition, act):
+        if cols * g < 9:
+            pl.when(condition())(act)
+        else:
+            act()
+
+    def where_needed(g, j, act):
+        def condition():
+            return jnp.logical_not((upper_only(g, j) & (z < half)) | (lower_only(g, j) & (z >= half)))
+
+        guarded(g, condition, act)
+
+    def where_comes(g, side, act):
+        def condition():
+            if side < 0:
+                return jnp.logical_not(lower_only(g, 0) & (z >= half))
+            return jnp.logical_not(upper_only(g, 0) & (z < half))
+
+        guarded(g, condition, act)
+
+    def pass_up(g, source, act):
+        def go():
+            guarded(g, lambda: jnp.logical_not(lower_only(g, 0) & (z + 1 >= half)), lambda: act(z_up(g, source)))
+
+        pl.when(z < depth - 1)(go)
+
+    def pass_down(g, source, act):
+        def go():
+            guarded(g, lambda: jnp.logical_not(upper_only(g, 0) & (z - 1 < half)), lambda: act(z_down(g, source)))
+
+        pl.when(z > 0)(go)
 
     def z_up(g, source):
         p = piece(g, 0, source)
@@ -214,60 +276,119 @@
         p = piece(g, via, source)
         return remote(p, p, diag_send.at[g, source], w_recv.at[g, 3, source], row, col_of[3 - via])
 
-    def to_core(g, j):
-        p = wg.at[cols * g + col_of[j], :, core]
-        return remote(p, p, core_send.at[g, j], core_recv.at[g, j], other_core, col)
-
-    def from_core(g, j):
-        p = wg.at[cols * g + col_of[j], :, 1 - core]
-        return remote(p, p, core_send.at[g, j], core_recv.at[g, j], other_core, col)
+    def to_core(g, j, source):
+        p = piece(g, j, source)
+        return remote(p, p, core_send.at[g, j, source], core_recv.at[g, j, source], other_core, col)
+
+    def own_to_core(g):
+        p = wg.at[pl.ds(g * cols, cols), z, core]
+        return remote(p, p, own_send.at[g], own_recv.at[g], other_core, col)
+
+    def from_core(g, j, source):
+        p = piece(g, j, source, 1 - core)
+        remote(p, p, core_send.at[g, j, source], core_recv.at[g, j, source], other_core, col).wait_recv()
+
+    def own_from_core(g):
+        p = wg.at[pl.ds(g * cols, cols), z, 1 - core]
+        remote(p, p, own_send.at[g], own_recv.at[g], other_core, col).wait_recv()
 
     def arrived(g, j, source):
         p = piece(g, j, source)
         remote(p, p, x_send.at[g, source], w_recv.at[g, j, source], row, col_of[1]).wait_recv()
 
-    def others(act):
-        for d in range(1, depth):
-            for side in (-1, 1):
-                source = z + side * d
-                pl.when((source >= 0) & (source < depth))(functools.partial(act, source, side, d))
-
-    def own_z(g):
-        pl.when(z < depth - 1)(lambda: z_up(g, z).start())
-        pl.when(z > 0)(lambda: z_down(g, z).start())
-
-    def z_phase(g):
-        def act(source, side, d):
-            arrived(g, 0, source)
-            if side < 0:
-                pl.when(z < depth - 1)(lambda: z_up(g, source).start())
-            else:
-                pl.when(z > 0)(lambda: z_down(g, source).start())
-            to_x(g, source).start()
-            to_y(g, source).start()
-
-        others(act)
-        to_core(g, 0).start()
-
-    def plane_phase(g):
+    def at_distance(d, act):
+        for side in (-1, 1):
+            source = z + side * d
+            pl.when((source >= 0) & (source < depth))(functools.partial(act, source, side))
+
+    def begin(copy):
+        copy.start()
+
+    def end(copy):
+        copy.wait_send()
+
+    def own_z(g, act=begin):
+        pass_up(g, z, act)
+        pass_down(g, z, act)
+
+    def pass_along(g, source, side, act):
+        if side < 0:
+            pass_up(g, source, act)
+        else:
+            pass_down(g, source, act)
+
+    def z_phase(g, d):
+        def act(source, side):
+            def come():
+                arrived(g, 0, source)
+                pass_along(g, source, side, begin)
+
+                def share():
+                    if not along_z(g):
+                        to_x(g, source).start()
+                        to_y(g, source).start()
+                    to_core(g, 0, source).start()
+
+                where_needed(g, 0, share)
+
+            where_comes(g, side, come)
+
+        at_distance(d, act)
+
+    def plane_phase(g, d):
         via = relay_via(g)
 
-        def act(source, side, d):
-            arrived(g, via, source)
-            to_diag(g, source).start()
-            arrived(g, 3 - via, source)
-
-        others(act)
-        to_core(g, 1).start()
-        to_core(g, 2).start()
-
-    def diag_phase(g):
-        others(lambda source, side, d: arrived(g, 3, source))
-        to_core(g, 3).start()
-
-    def core_phase(g):
-        for j in range(4):
-            from_core(g, j).wait_recv()
+        def act(source, side):
+            def first():
+                arrived(g, via, source)
+                to_diag(g, source).start()
+                to_core(g, via, source).start()
+
+            def second():
+                arrived(g, 3 - via, source)
+                to_core(g, 3 - via, source).start()
+
+            where_needed(g, via, first)
+            where_needed(g, 3 - via, second)
+
+        at_distance(d, act)
+
+    def diag_phase(g, d):
+        def act(source, side):
+            def come():
+                arrived(g, 3, source)
+                to_core(g, 3, source).start()
+
+            where_needed(g, 3, come)
+
+        at_distance(d, act)
+
+    def core_phase(g, d):
+        def act(source, side):
+            for j in range(1 if along_z(g) else 4):
+                where_needed(g, j, lambda j=j: from_core(g, j, source))
+
+        at_distance(d, act)
+
+    def ended(g, d):
+        def act(source, side):
+            where_comes(g, side, lambda: pass_along(g, source, side, end))
+
+            def shared():
+                if not along_z(g):
+                    to_x(g, source).wait_send()
+                    to_y(g, source).wait_send()
+                to_core(g, 0, source).wait_send()
+
+            where_needed(g, 0, shared)
+            if along_z(g):
+                return
+            via = relay_via(g)
+            where_needed(g, via, lambda: to_diag(g, source).wait_send())
+            for j in range(1, 4):
+                where_needed(g, j, lambda j=j: to_core(g, j, source).wait_send())
+
+        at_distance(d, act)
 
     tile_copies = [
         remote(x_ref, xin.at[0], tile_send.at[0], tile_recv.at[0], far_row, col),
@@ -351,69 +472,70 @@
     hooks = {}
     first_plain, centre, second_plain = 9, 18, 19
 
+    long = groups - 1
+    long_at = [LONG_START + Z_LAG * n for n in range(depth)]
+    own_z(0)
+    tile_copies[1].start()
+    own_z(1)
     tile_copies[0].start()
-    tile_copies[1].start()
-    own_z(0)
-    own_z(1)
+    for g in range(2, AHEAD):
+        own_z(g)
     ready = 0
     stage = 0
-    for step in range(groups + 3):
-        if step < groups:
-            z_phase(step)
-            if step + 2 < groups:
-                own_z(step + 2)
-        if step == 1:
+    for g in range(groups):
+        own_to_core(g).start()
+    delays = (0, PLANE_LAG, PLANE_LAG + DIAG_LAG, PLANE_LAG + DIAG_LAG + CORE_LAG)
+    whole_lag = Z_LAG * (depth - 2) + delays[-1]
+    for step in range(long + whole_lag):
+        for lag, phase in zip(delays, (z_phase, plane_phase, diag_phase, core_phase)):
+            for d in range(1, depth):
+                g = step - lag - Z_LAG * (d - 1)
+                if 0 <= g < long:
+                    phase(g, d)
+            if lag == 0:
+                if step + AHEAD < long:
+                    own_z(step + AHEAD)
+                if step == max(LONG_START - 2, 0):
+                    own_z(long)
+                for d in range(1, depth):
+                    if step == long_at[d - 1]:
+                        z_phase(long, d)
+                    if step == long_at[d - 1] + CORE_LAG:
+                        core_phase(long, d)
+        if step == TILE_STEP:
             tile_copies[0].wait_recv()
             tile_copies[2].start()
-        if 0 <= step - 1 < groups:
-            plane_phase(step - 1)
-        if 0 <= step - 2 < groups:
-            diag_phase(step - 2)
-        if step - 3 < 0:
+        whole = step - whole_lag
+        if whole < 0:
             continue
-        core_phase(step - 3)
-        ready = (step - 2) * cols
+        own_from_core(whole)
+        ready = (whole + 1) * cols
+        if whole == long - 1:
+            own_from_core(long)
+            ready = taps
         if stage == 0 and ready >= first_plain:
             first_block()
             stage = 1
         elif stage == 1:
-            split = min(ready, centre) - first_plain
+            done = min(ready, centre) - first_plain
             take_halo(0)
-            current[...] = radar_ref[...] + plain(0, split, first_plain)
-            done = split
+            current[...] += plain(0, done, first_plain)
             stage = 2
         if stage == 2 and ready > centre:
-            current[...] += plain(done, 9, first_plain)
+            if done < 9:
+                current[...] += plain(done, 9, first_plain)
             normalize(1, product(current[...].astype(jnp.bfloat16), centre))
             stage = 3
-        elif stage == 3:
-            split = min(ready, taps) - second_plain
-            take_halo(1)
-            current[...] += plain(0, split, second_plain)
-            done = split
-            stage = 4
-        elif stage == 4:
-            o_ref[...] = current[...] + plain(done, 9, second_plain)
-            stage = 5
+    take_halo(1)
+    o_ref[...] = current[...] + plain(0, 9, second_plain)
 
     for copy in tile_copies:
         copy.wait_send()
     for g in range(groups):
-        pl.when(z < depth - 1)(lambda: z_up(g, z).wait_send())
-        pl.when(z > 0)(lambda: z_down(g, z).wait_send())
-
-        def act(source, side, d):
-            if side < 0:
-                pl.when(z < depth - 1)(lambda: z_up(g, source).wait_send())
-            else:
-                pl.when(z > 0)(lambda: z_down(g, source).wait_send())
-            to_x(g, source).wait_send()
-            to_y(g, source).wait_send()
-            to_diag(g, source).wait_send()
-
-        others(act)
-        for j in range(4):
-            to_core(g, j).wait_send()
+        own_z(g, end)
+        for d in range(1, depth):
+            ended(g, d)
+        own_to_core(g).wait_send()
     for b in range(2):
         for n, (dr, dc, ok) in enumerate(neighbours):
             pl.when(ok)(lambda: halo_copy(b, n).wait_send())
@@ -424,19 +546,22 @@
     part = kernels.shape[-1]
     depth = rows // 2
     flat = jnp.swapaxes(kernels.reshape(BLOCKS * 2, 9, channels, part), 2, 3)
-    weights = jnp.concatenate([flat[0], flat[1], flat[2, 4:5], flat[3]])
-    taps = weights.shape[0]
+    weights = flat
+    parts = ((0, 0, 9), (1, 0, 9), (2, 4, 1), (3, 0, 9))
+    taps = sum(count for _, _, count in parts)
     groups = taps // cols
     flat_radar = radar_field.reshape(th * tw, channels)
     vmem = pl.BlockSpec(memory_space=pltpu.VMEM)
     dma = pltpu.SemaphoreType.DMA
     out = pl.pallas_call(
-        functools.partial(block_kernel, rows, cols, th, tw, taps),
+        functools.partial(block_kernel, rows, cols, th, tw, taps, parts),
         out_shape=jax.ShapeDtypeStruct((th * tw, channels), jnp.float32),
-        in_specs=[vmem, pl.BlockSpec(memory_space=pl.ANY), vmem, vmem],
+        in_specs=[pl.BlockSpec(memory_space=pltpu.HBM)] * 3,
         out_specs=vmem,
         scratch_shapes=[
             pltpu.VMEM((taps, depth, 2, part, channels), jnp.bfloat16),
+            pltpu.VMEM((th * tw, channels), jnp.bfloat16),
+            pltpu.VMEM(norm_gain_weights.shape, jnp.float32),
             pltpu.VMEM((3, th * tw, channels), jnp.bfloat16),
             pltpu.VMEM((2, th, tw, channels), jnp.bfloat16),
             pltpu.VMEM((2, 2, th, channels), jnp.bfloat16),
@@ -444,24 +569,27 @@
             pltpu.VMEM((2, 2, 3, th, channels), jnp.bfloat16),
             pltpu.VMEM((th + 2, -(-(tw + 2) // 8) * 8, channels), jnp.float32),
             pltpu.VMEM((th * tw, channels), jnp.float32),
-            dma((groups,)),
+            dma((2,)),
+            dma((len(parts),)),
             dma((groups, 4, depth)),
             dma((groups, depth)),
             dma((groups, depth)),
             dma((groups, depth)),
             dma((groups, depth)),
             dma((groups, depth)),
-            dma((groups, 4)),
-            dma((groups, 4)),
+            dma((groups, 4, depth)),
+            dma((groups, 4, depth)),
+            dma((groups,)),
+            dma((groups,)),
             dma((3,)),
             dma((3,)),
             dma((2, 8)),
             dma((2, 8)),
         ],
         compiler_params=pltpu.CompilerParams(
-            collective_id=0, has_side_effects=True, vmem_limit_bytes=48 * 1024 * 1024
+            collective_id=0, has_side_effects=True, vmem_limit_bytes=67_000_000
         ),
-    )(flat_radar.astype(jnp.bfloat16), weights, flat_radar, norm_gain_weights)
+    )(weights, flat_radar, norm_gain_weights)
     return out.reshape(th, tw, channels)
 
 

time: 61.3 us -> 56 us (0.914)
  Pallas kernels: 58.1 us -> 54.2 us
  local copies, waits for them, and re-layouts: 2.78 us -> 1.62 us
    pallas_call x1, Pallas kernels: 58.1 us -> 54.2 us  [one_kernel(): pl.pallas_call(functools.partial(block_kernel, rows, cols, th, tw, taps,...]
    squeeze x2 -> x0, local copies, waits for them, and re-layouts: 2.09 us -> none  [one_kernel(): weights = jnp.concatenate([flat[0], flat[1], flat[2, 4:5], flat[3]])]
    unnamed x5 -> x1, local copies, waits for them, and re-layouts: 0.69 us -> 1.62 us
where the time goes in v2:
time: 56 us; the launch traced here: 55.8 us
  Pallas kernels  54.2 us (97%)
  local copies, waits for them, and re-layouts  1.62 us (3%)
    pallas_call x1, Pallas kernels, one_kernel(): pl.pallas_call(functools.partial(block_kernel, rows, cols, th, tw, taps,...  54.2 us
    unnamed x1, local copies, waits for them, and re-layouts  1.62 us

profile of v2, /device:TPU:0, one launch (start us, length us, event | category | flops | bytes accessed | tf_op | source)
XLA Modules:
  0.0 55.8 jit_solution(13741444177443679436)
XLA Ops:
  0.0 54.2 %shard_map.37 = f32[128,384]{1,0:T(8,128)} custom-call(bf16[4,9,48,384]{3,2,1,0:T(8,128)(2,1)} %bitcast.5, f32[128,384]{1,0:T(8,128)} %bitcast.7, f32[2,384]{1,0:T(2,128)} %gain_hbm.1), custom_call_target="tpu_custom_call" | custom-call | tf_op jit(solution)/shard_map/pallas_call | solution.py:556
  54.2 1.6 %copy.5 = f32[8,16,384]{2,1,0:T(8,128)} copy(f32[8,16,384]{2,1,0:T(8,128)} %bitcast.6) | data formatting | bytes 393216
